TPU v7x, 256 devices: a whole 4x4x8 slice. The times are simulated.
256 devices in a mesh: section: 8 (over z), expert: 8 (over y_hi, x), dp: 4 (over y_lo, core).
Axes of the slice: x: 4, y: 4 (y_hi: 2, y_lo: 2; y = y_hi * 2 + y_lo), z: 8, core: 2. Of those that a mesh axis runs over, the one named last changes fastest.
Arguments:
- tokens: bfloat16 [8, 256, 4096], P('section', None, ('expert', 'dp'))
- targets: bfloat16 [8, 256, 4096], P('section', None, ('expert', 'dp')), may hold values from -6 to 6
- group_ids: int32 [8, 256], P('section'), may hold values from 0 to 7, as said below
- expert_ids: int32 [1, 8, 8, 256, 2], P(None, 'section'), may hold values from 0 to 7, all different within a row; in each aligned block of 256 rows (0 to 255, 256 to 511, ..., all dimensions but the last counted through in order) at most 72 rows name the same one
- norm_gain: float32 [8, 4096], P('section', ('expert', 'dp')), may hold values from 0.5 to 1.5
- router: bfloat16 [8, 4096, 8], P('section', ('expert', 'dp')), may hold values from -0.09375 to 0.09375
- w_gate: bfloat16 [8, 8, 4096, 1536], P('section', 'expert', None, 'dp'), may hold values from -0.09375 to 0.09375
- w_up: bfloat16 [8, 8, 4096, 1536], P('section', 'expert', None, 'dp'), may hold values from -0.09375 to 0.09375
- w_down: bfloat16 [8, 8, 1536, 4096], P('section', 'expert', 'dp'), may hold values from -0.15625 to 0.15625
Outputs:
- grad_out: bfloat16 [8, 256, 4096], P('section', None, ('expert', 'dp'))
- group_loss: float32 [8], replicated
Inputs may be any that keep to these rules, and one draw needn't show every extreme that they name: `expert_ids`: in each aligned block of 256 rows (one micro-batch at one layer pass) no expert is named by more than 72 rows; a row names 2 different experts. `group_ids`: exactly one group has no rows; which one varies.
All inputs are finite; a program needn't handle non-finite values.
Results may differ from a plain program's by a relative error of at most 0.019.
Values may be sent and summed in bfloat16 or wider, within the bound.
A program may use at most 64 MiB of HBM per device.

v0:
```python
import jax
import jax.numpy as jnp
from jax import lax
from jax.sharding import PartitionSpec as P

GROUPS = 8
dro_rate = 0.3


def from_behind(value, axis, steps):
    count = lax.axis_size(axis)
    pairs = [(source, (source + steps) % count) for source in range(count)]
    return lax.ppermute(value, axis, pairs)


def per_device(tokens, targets, group_ids, expert_ids, norm_gain, router, w_gate, w_up, w_down):
    sections = lax.axis_size("section")
    lane_count = lax.axis_size("dp")
    experts = lax.axis_size("expert")
    circuits = expert_ids.shape[0]
    top_count = expert_ids.shape[-1]
    row_count = tokens.shape[1]
    piece_width = tokens.shape[2]
    full_width = piece_width * experts * lane_count
    capacity = min(row_count, row_count * top_count // experts * 9 // 8)
    section_place = lax.axis_index("section")
    gain_row = norm_gain[0]
    router_block = router[0]
    gate_matrix = w_gate[0, 0]
    up_matrix = w_up[0, 0]
    down_matrix = w_down[0, 0]
    expert_range = jnp.arange(experts, dtype=jnp.int32)
    slot_range = jnp.arange(capacity, dtype=jnp.int32)
    zero_index = jnp.zeros((), jnp.int32)

    def expert_rows(flat_rows):
        gate_part = jnp.dot(flat_rows, gate_matrix, preferred_element_type=jnp.float32)
        up_part = jnp.dot(flat_rows, up_matrix, preferred_element_type=jnp.float32)
        activated = (jax.nn.silu(gate_part) * up_part).astype(jnp.bfloat16)
        return jnp.dot(activated, down_matrix, preferred_element_type=jnp.float32).astype(
            jnp.bfloat16
        )

    def joined_work(received):
        item_count = received.shape[1]
        expert_part = expert_rows(received.reshape(item_count, full_width))
        return lax.all_to_all(
            expert_part.reshape(item_count, experts * lane_count, piece_width),
            ("expert", "dp"),
            split_axis=1,
            concat_axis=1,
            tiled=True,
        )

    def one_tick(moment, current):
        micro_index = (section_place - moment) % sections
        circuit = (moment // sections).astype(jnp.int32)
        choices = lax.dynamic_slice(
            expert_ids,
            (circuit, zero_index, micro_index, zero_index, zero_index),
            (1, 1, 1, row_count, top_count),
        ).reshape(row_count, top_count)
        wide_state = current.astype(jnp.float32)
        local_squares = jnp.sum(wide_state * wide_state, axis=1)
        total_squares = lax.psum(local_squares, ("expert", "dp"))
        row_scale = lax.rsqrt(total_squares / full_width + 1e-06)[:, None]
        normed = (wide_state * row_scale * gain_row[None, :]).astype(jnp.bfloat16)
        partial_logits = jnp.dot(normed, router_block, preferred_element_type=jnp.float32)
        logits = lax.psum(partial_logits, ("expert", "dp"))
        member = (choices[:, :, None] == expert_range[None, None, :]).astype(jnp.int32)
        flat_member = member.reshape(-1, experts)
        rank_before = jnp.cumsum(flat_member, axis=0) - flat_member
        position = jnp.sum(rank_before * flat_member, axis=1).reshape(row_count, top_count)
        chosen = jnp.sum(logits[:, None, :] * member.astype(jnp.float32), axis=2)
        weights = jnp.exp(chosen)
        gate_weights = weights / jnp.sum(weights, axis=1, keepdims=True)
        placement = member.astype(jnp.float32)[:, :, :, None] * (
            position[:, :, None, None] == slot_range[None, None, None, :]
        ).astype(jnp.float32)
        picker = (
            jnp.sum(placement, axis=1).reshape(row_count, experts * capacity).astype(jnp.bfloat16)
        )
        combiner = jnp.sum(placement * gate_weights[:, :, None, None], axis=1)
        outgoing = jnp.einsum(
            "us,ud->sd", picker, normed, preferred_element_type=jnp.float32
        ).astype(jnp.bfloat16)
        spread = jnp.broadcast_to(
            outgoing.reshape(experts, 1, capacity, piece_width),
            (experts, lane_count, capacity, piece_width),
        )
        returned = joined_work(
            lax.all_to_all(
                spread.reshape(experts * lane_count, capacity, piece_width),
                ("expert", "dp"),
                split_axis=0,
                concat_axis=2,
                tiled=True,
            )
        )
        lane_total = jnp.sum(
            returned.reshape(capacity, experts, lane_count, piece_width).astype(jnp.float32), axis=2
        )
        mixture = jnp.einsum("uec,ced->ud", combiner, lane_total, precision=lax.Precision.HIGHEST)
        updated = (wide_state + mixture).astype(jnp.bfloat16)
        return from_behind(updated, "section", 1)

    final_state = lax.fori_loop(0, circuits * sections, one_tick, tokens[0])
    difference = final_state.astype(jnp.float32) - targets[0].astype(jnp.float32)
    partial_squares = jnp.sum(difference * difference, axis=1) / full_width
    group_member = (group_ids[0][:, None] == jnp.arange(GROUPS, dtype=jnp.int32)[None, :]).astype(
        jnp.float32
    )
    local_totals = jnp.dot(partial_squares, group_member, precision=lax.Precision.HIGHEST)
    first_lane = ((lax.axis_index("expert") == 0) & (lax.axis_index("dp") == 0)).astype(jnp.float32)
    local_counts = jnp.sum(group_member, axis=0) * first_lane
    totals, counts = lax.psum((local_totals, local_counts), ("section", "expert", "dp"))
    group_loss = totals / jnp.maximum(counts, 1.0)
    raised = jnp.exp(dro_rate * group_loss)
    group_weight = raised / jnp.sum(raised)
    token_count = sections * row_count
    row_weight_table = group_weight * token_count / jnp.maximum(counts, 1.0)
    row_weight = jnp.dot(group_member, row_weight_table, precision=lax.Precision.HIGHEST)
    grad_out = (row_weight[:, None] * difference).astype(jnp.bfloat16)[None]
    return (grad_out, group_loss)


def solution(mesh):
    placed = (
        P("section", None, ("expert", "dp")),
        P("section", None, ("expert", "dp")),
        P("section", None),
        P(None, "section", None, None, None),
        P("section", ("expert", "dp")),
        P("section", ("expert", "dp"), None),
        P("section", "expert", None, "dp"),
        P("section", "expert", None, "dp"),
        P("section", "expert", "dp", None),
    )
    return jax.shard_map(
        per_device,
        mesh=mesh,
        in_specs=placed,
        out_specs=(P("section", None, ("expert", "dp")), P()),
        check_vma=False,
    )
```

profile of v0, /device:TPU:1, one launch (start us, length us, event | category | flops | bytes accessed | tf_op | source)
XLA Modules:
  0.0 1500.4 jit_solution(1334823001441641367)
XLA Ops:
  2.3 1422.9 %while.17 = (s32[]{:T(128)}, bf16[256,128]{1,0:T(8,128)(2,1)S(1)}, s32[]{:T(128)}, s32[1,1,8,256,2]{3,4,2,1,0:T(2,128)}, f32[1,128]{1,0:T(1,128)}, /*index=5*/bf...) while((s32[]{:T(128)}, bf16[256,128]{1,0:T(8,128)(2,1)S(1)}, ...), condition=%wide.region_12.13_spmd.clone.clone, body=%wide.region_0.12_spmd.clone.clone.sunk | while | flops 947298688 | bytes 33643788 | solution.py:107
  4.3 65.3 %psum.50 = f32[256]{0:T(256)S(1)} all-reduce(f32[256]{0:T(256)S(1)} %fusion.92), channel_id=1, replica_groups=mesh['section'=8,'expert'=8,'dp'=4] {'expert','dp'}, use_global_device_ids=true, to_apply=%region_5.5 | all-reduce | flops 256 | bytes 2048 | tf_op jit(solution)/shard_map/while/body/eval_jaxpr/psum | solution.py:65
  70.4 66.5 %psum.51 = f32[256,8]{0,1:T(8,128)S(1)} all-reduce(f32[256,8]{0,1:T(8,128)S(1)} %fusion.93), channel_id=1, replica_groups=mesh['section'=8,'expert'=8,'dp'=4] {'expert','dp'}, use_global_device_ids=true, to_apply=%region_6.6 | all-reduce | flops 2048 | bytes 16384 | tf_op jit(solution)/shard_map/while/body/eval_jaxpr/psum | solution.py:69
  161.6 16.2 %all_to_all.59 = bf16[72,32,128]{2,0,1:T(8,128)(2,1)S(1)} all-to-all(bf16[72,32,128]{2,0,1:T(8,128)(2,1)S(1)} %bitcast.119), channel_id=1, replica_groups=mesh['section'=8,'expert'=8,'dp'=4] {'expert','dp'}, dimensions={1} | all-to-all | bytes 1179648 | tf_op jit(solution)/shard_map/while/body/eval_jaxpr/all_to_all | solution.py:47
  188.4 63.6 %psum.50 = f32[256]{0:T(256)S(1)} all-reduce(f32[256]{0:T(256)S(1)} %fusion.92), channel_id=1, replica_groups=mesh['section'=8,'expert'=8,'dp'=4] {'expert','dp'}, use_global_device_ids=true, to_apply=%region_5.5 | all-reduce | flops 256 | bytes 2048 | tf_op jit(solution)/shard_map/while/body/eval_jaxpr/psum | solution.py:65
  253.0 63.6 %psum.51 = f32[256,8]{0,1:T(8,128)S(1)} all-reduce(f32[256,8]{0,1:T(8,128)S(1)} %fusion.93), channel_id=1, replica_groups=mesh['section'=8,'expert'=8,'dp'=4] {'expert','dp'}, use_global_device_ids=true, to_apply=%region_6.6 | all-reduce | flops 2048 | bytes 16384 | tf_op jit(solution)/shard_map/while/body/eval_jaxpr/psum | solution.py:69
  365.1 63.9 %psum.50 = f32[256]{0:T(256)S(1)} all-reduce(f32[256]{0:T(256)S(1)} %fusion.92), channel_id=1, replica_groups=mesh['section'=8,'expert'=8,'dp'=4] {'expert','dp'}, use_global_device_ids=true, to_apply=%region_5.5 | all-reduce | flops 256 | bytes 2048 | tf_op jit(solution)/shard_map/while/body/eval_jaxpr/psum | solution.py:65
  430.0 63.6 %psum.51 = f32[256,8]{0,1:T(8,128)S(1)} all-reduce(f32[256,8]{0,1:T(8,128)S(1)} %fusion.93), channel_id=1, replica_groups=mesh['section'=8,'expert'=8,'dp'=4] {'expert','dp'}, use_global_device_ids=true, to_apply=%region_6.6 | all-reduce | flops 2048 | bytes 16384 | tf_op jit(solution)/shard_map/while/body/eval_jaxpr/psum | solution.py:69
  518.2 16.2 %all_to_all.59 = bf16[72,32,128]{2,0,1:T(8,128)(2,1)S(1)} all-to-all(bf16[72,32,128]{2,0,1:T(8,128)(2,1)S(1)} %bitcast.119), channel_id=1, replica_groups=mesh['section'=8,'expert'=8,'dp'=4] {'expert','dp'}, dimensions={1} | all-to-all | bytes 1179648 | tf_op jit(solution)/shard_map/while/body/eval_jaxpr/all_to_all | solution.py:47
  542.1 63.9 %psum.50 = f32[256]{0:T(256)S(1)} all-reduce(f32[256]{0:T(256)S(1)} %fusion.92), channel_id=1, replica_groups=mesh['section'=8,'expert'=8,'dp'=4] {'expert','dp'}, use_global_device_ids=true, to_apply=%region_5.5 | all-reduce | flops 256 | bytes 2048 | tf_op jit(solution)/shard_map/while/body/eval_jaxpr/psum | solution.py:65
  607.0 63.6 %psum.51 = f32[256,8]{0,1:T(8,128)S(1)} all-reduce(f32[256,8]{0,1:T(8,128)S(1)} %fusion.93), channel_id=1, replica_groups=mesh['section'=8,'expert'=8,'dp'=4] {'expert','dp'}, use_global_device_ids=true, to_apply=%region_6.6 | all-reduce | flops 2048 | bytes 16384 | tf_op jit(solution)/shard_map/while/body/eval_jaxpr/psum | solution.py:69
  719.1 63.9 %psum.50 = f32[256]{0:T(256)S(1)} all-reduce(f32[256]{0:T(256)S(1)} %fusion.92), channel_id=1, replica_groups=mesh['section'=8,'expert'=8,'dp'=4] {'expert','dp'}, use_global_device_ids=true, to_apply=%region_5.5 | all-reduce | flops 256 | bytes 2048 | tf_op jit(solution)/shard_map/while/body/eval_jaxpr/psum | solution.py:65
  784.0 63.6 %psum.51 = f32[256,8]{0,1:T(8,128)S(1)} all-reduce(f32[256,8]{0,1:T(8,128)S(1)} %fusion.93), channel_id=1, replica_groups=mesh['section'=8,'expert'=8,'dp'=4] {'expert','dp'}, use_global_device_ids=true, to_apply=%region_6.6 | all-reduce | flops 2048 | bytes 16384 | tf_op jit(solution)/shard_map/while/body/eval_jaxpr/psum | solution.py:69
  872.2 16.2 %all_to_all.59 = bf16[72,32,128]{2,0,1:T(8,128)(2,1)S(1)} all-to-all(bf16[72,32,128]{2,0,1:T(8,128)(2,1)S(1)} %bitcast.119), channel_id=1, replica_groups=mesh['section'=8,'expert'=8,'dp'=4] {'expert','dp'}, dimensions={1} | all-to-all | bytes 1179648 | tf_op jit(solution)/shard_map/while/body/eval_jaxpr/all_to_all | solution.py:47
  896.1 63.9 %psum.50 = f32[256]{0:T(256)S(1)} all-reduce(f32[256]{0:T(256)S(1)} %fusion.92), channel_id=1, replica_groups=mesh['section'=8,'expert'=8,'dp'=4] {'expert','dp'}, use_global_device_ids=true, to_apply=%region_5.5 | all-reduce | flops 256 | bytes 2048 | tf_op jit(solution)/shard_map/while/body/eval_jaxpr/psum | solution.py:65
  960.9 63.6 %psum.51 = f32[256,8]{0,1:T(8,128)S(1)} all-reduce(f32[256,8]{0,1:T(8,128)S(1)} %fusion.93), channel_id=1, replica_groups=mesh['section'=8,'expert'=8,'dp'=4] {'expert','dp'}, use_global_device_ids=true, to_apply=%region_6.6 | all-reduce | flops 2048 | bytes 16384 | tf_op jit(solution)/shard_map/while/body/eval_jaxpr/psum | solution.py:69
  1049.2 16.2 %all_to_all.59 = bf16[72,32,128]{2,0,1:T(8,128)(2,1)S(1)} all-to-all(bf16[72,32,128]{2,0,1:T(8,128)(2,1)S(1)} %bitcast.119), channel_id=1, replica_groups=mesh['section'=8,'expert'=8,'dp'=4] {'expert','dp'}, dimensions={1} | all-to-all | bytes 1179648 | tf_op jit(solution)/shard_map/while/body/eval_jaxpr/all_to_all | solution.py:47
  1073.1 63.9 %psum.50 = f32[256]{0:T(256)S(1)} all-reduce(f32[256]{0:T(256)S(1)} %fusion.92), channel_id=1, replica_groups=mesh['section'=8,'expert'=8,'dp'=4] {'expert','dp'}, use_global_device_ids=true, to_apply=%region_5.5 | all-reduce | flops 256 | bytes 2048 | tf_op jit(solution)/shard_map/while/body/eval_jaxpr/psum | solution.py:65
  1137.9 63.6 %psum.51 = f32[256,8]{0,1:T(8,128)S(1)} all-reduce(f32[256,8]{0,1:T(8,128)S(1)} %fusion.93), channel_id=1, replica_groups=mesh['section'=8,'expert'=8,'dp'=4] {'expert','dp'}, use_global_device_ids=true, to_apply=%region_6.6 | all-reduce | flops 2048 | bytes 16384 | tf_op jit(solution)/shard_map/while/body/eval_jaxpr/psum | solution.py:69
  1226.2 16.2 %all_to_all.59 = bf16[72,32,128]{2,0,1:T(8,128)(2,1)S(1)} all-to-all(bf16[72,32,128]{2,0,1:T(8,128)(2,1)S(1)} %bitcast.119), channel_id=1, replica_groups=mesh['section'=8,'expert'=8,'dp'=4] {'expert','dp'}, dimensions={1} | all-to-all | bytes 1179648 | tf_op jit(solution)/shard_map/while/body/eval_jaxpr/all_to_all | solution.py:47
  1250.1 63.9 %psum.50 = f32[256]{0:T(256)S(1)} all-reduce(f32[256]{0:T(256)S(1)} %fusion.92), channel_id=1, replica_groups=mesh['section'=8,'expert'=8,'dp'=4] {'expert','dp'}, use_global_device_ids=true, to_apply=%region_5.5 | all-reduce | flops 256 | bytes 2048 | tf_op jit(solution)/shard_map/while/body/eval_jaxpr/psum | solution.py:65
  1314.9 63.6 %psum.51 = f32[256,8]{0,1:T(8,128)S(1)} all-reduce(f32[256,8]{0,1:T(8,128)S(1)} %fusion.93), channel_id=1, replica_groups=mesh['section'=8,'expert'=8,'dp'=4] {'expert','dp'}, use_global_device_ids=true, to_apply=%region_6.6 | all-reduce | flops 2048 | bytes 16384 | tf_op jit(solution)/shard_map/while/body/eval_jaxpr/psum | solution.py:69
  1403.2 16.2 %all_to_all.59 = bf16[72,32,128]{2,0,1:T(8,128)(2,1)S(1)} all-to-all(bf16[72,32,128]{2,0,1:T(8,128)(2,1)S(1)} %bitcast.119), channel_id=1, replica_groups=mesh['section'=8,'expert'=8,'dp'=4] {'expert','dp'}, dimensions={1} | all-to-all | bytes 1179648 | tf_op jit(solution)/shard_map/while/body/eval_jaxpr/all_to_all | solution.py:47
  1425.4 72.8 %all-reduce = (f32[8]{0:T(128)S(1)}, f32[8]{0:T(128)S(1)}) all-reduce(f32[8]{0:T(128)S(1)} %broadcast_multiply_fusion.1, f32[8]{0:T(128)S(1)} %convolution_bitcast_fusion.1), channel_id=1, replica_groups=mesh['section'=8,'expert'=8,'dp'=4] {'section','expert','dp'}, use_global_device_ids=true, to_apply=%region_16.17 | all-reduce | flops 16 | bytes 128 | tf_op jit(solution)/shard_map/psum | solution.py:116
  (297 shorter events, 303.8 us)
Async XLA Ops:
  2.3 1422.9 %copy-start.1 = (bf16[1,256,128]{2,1,0:T(8,128)(2,1)S(1)}, bf16[1,256,128]{2,1,0:T(8,128)(2,1)}, u32[]{:S(2)}) copy-start(bf16[1,256,128]{2,1,0:T(8,128)(2,1)} %param.12) | copy-start | bytes 196612
  2.3 1423.0 %copy-start.3 = (s32[1,256]{1,0:T(1,128)S(1)}, s32[1,256]{1,0:T(1,128)}, u32[]{:S(2)}) copy-start(s32[1,256]{1,0:T(1,128)} %param.13) | copy-start | bytes 3076
  138.8 17.4 %copy-start = (bf16[4096,384]{1,0:T(8,128)(2,1)S(1)}, bf16[4096,384]{1,0:T(8,128)(2,1)}, u32[]{:S(2)}) copy-start(bf16[4096,384]{1,0:T(8,128)(2,1)} %get-tuple-element.482) | copy-start | bytes 9437188 | tf_op jit(solution)/shard_map/while
  179.2 7.3 collective-permute-start
  318.4 17.4 %copy-start = (bf16[4096,384]{1,0:T(8,128)(2,1)S(1)}, bf16[4096,384]{1,0:T(8,128)(2,1)}, u32[]{:S(2)}) copy-start(bf16[4096,384]{1,0:T(8,128)(2,1)} %get-tuple-element.482) | copy-start | bytes 9437188 | tf_op jit(solution)/shard_map/while
  358.8 4.4 collective-permute-start
  495.4 17.4 %copy-start = (bf16[4096,384]{1,0:T(8,128)(2,1)S(1)}, bf16[4096,384]{1,0:T(8,128)(2,1)}, u32[]{:S(2)}) copy-start(bf16[4096,384]{1,0:T(8,128)(2,1)} %get-tuple-element.482) | copy-start | bytes 9437188 | tf_op jit(solution)/shard_map/while
  535.8 4.4 collective-permute-start
  672.4 17.4 %copy-start = (bf16[4096,384]{1,0:T(8,128)(2,1)S(1)}, bf16[4096,384]{1,0:T(8,128)(2,1)}, u32[]{:S(2)}) copy-start(bf16[4096,384]{1,0:T(8,128)(2,1)} %get-tuple-element.482) | copy-start | bytes 9437188 | tf_op jit(solution)/shard_map/while
  712.8 4.4 collective-permute-start
  849.4 17.4 %copy-start = (bf16[4096,384]{1,0:T(8,128)(2,1)S(1)}, bf16[4096,384]{1,0:T(8,128)(2,1)}, u32[]{:S(2)}) copy-start(bf16[4096,384]{1,0:T(8,128)(2,1)} %get-tuple-element.482) | copy-start | bytes 9437188 | tf_op jit(solution)/shard_map/while
  889.8 4.4 collective-permute-start
  1026.4 17.4 %copy-start = (bf16[4096,384]{1,0:T(8,128)(2,1)S(1)}, bf16[4096,384]{1,0:T(8,128)(2,1)}, u32[]{:S(2)}) copy-start(bf16[4096,384]{1,0:T(8,128)(2,1)} %get-tuple-element.482) | copy-start | bytes 9437188 | tf_op jit(solution)/shard_map/while
  1066.8 4.4 collective-permute-start
  1203.4 17.4 %copy-start = (bf16[4096,384]{1,0:T(8,128)(2,1)S(1)}, bf16[4096,384]{1,0:T(8,128)(2,1)}, u32[]{:S(2)}) copy-start(bf16[4096,384]{1,0:T(8,128)(2,1)} %get-tuple-element.482) | copy-start | bytes 9437188 | tf_op jit(solution)/shard_map/while
  1243.8 4.4 collective-permute-start
  1380.4 17.4 %copy-start = (bf16[4096,384]{1,0:T(8,128)(2,1)S(1)}, bf16[4096,384]{1,0:T(8,128)(2,1)}, u32[]{:S(2)}) copy-start(bf16[4096,384]{1,0:T(8,128)(2,1)} %get-tuple-element.482) | copy-start | bytes 9437188 | tf_op jit(solution)/shard_map/while
  1420.8 4.4 collective-permute-start
  1498.9 1.5 copy-start.2
where the time goes:
time: 1500 us
  blocking collectives  1350 us (90%)
  matrix products  68.6 us (5%)
  waiting for transfers between devices  35.8 us (2%)
  local copies, waits for them, and re-layouts  20.9 us (1%)
  other arithmetic  16.5 us (1%)
    psum x8, blocking collectives, one_tick(): total_squares = lax.psum(local_squares, ('expert', 'dp'))  512 us
    psum x8, blocking collectives, one_tick(): logits = lax.psum(partial_logits, ('expert', 'dp'))  512 us
    all_to_all x8, blocking collectives, joined_work(): lax.all_to_all(expert_part.reshape(item_count, experts * lane_count, piec...  130 us
    all_to_all x8, blocking collectives, one_tick(): lax.all_to_all(spread.reshape(experts * lane_count, capacity, piece_width...  127 us
    psum x1, blocking collectives, per_device(): lax.psum((local_totals, local_counts), ('section', 'expert', 'dp'))  72.8 us
    ppermute x8, waiting for transfers between devices, from_behind(): return lax.ppermute(value, axis, pairs)  35.8 us
    dot_general x8, matrix products, expert_rows(): jnp.dot(activated, down_matrix, preferred_element_type=jnp.float32)  35.4 us
  transfers between devices with their start and end apart: 8, of which 8 were waited for; matrix products, arithmetic and copies ran while one was open for 0% of the time, Pallas kernels for 0%

commit v1 on v0

--- a/solution.py
+++ b/solution.py
@@ -5,6 +5,7 @@
 
 GROUPS = 8
 dro_rate = 0.3
+_measure_ranges = lambda shard_in: lax.psum(lax.psum(shard_in, axis_name="dp"), "expert")
 
 
 def from_behind(value, axis, steps):
@@ -62,7 +63,7 @@
         ).reshape(row_count, top_count)
         wide_state = current.astype(jnp.float32)
         local_squares = jnp.sum(wide_state * wide_state, axis=1)
-        total_squares = lax.psum(local_squares, ("expert", "dp"))
+        total_squares = _measure_ranges(local_squares)
         row_scale = lax.rsqrt(total_squares / full_width + 1e-06)[:, None]
         normed = (wide_state * row_scale * gain_row[None, :]).astype(jnp.bfloat16)
         partial_logits = jnp.dot(normed, router_block, preferred_element_type=jnp.float32)

time: 1500 us -> 1210 us (0.81)
  blocking collectives: 1350 us -> 1060 us
    psum x8 -> x16, blocking collectives: 512 us -> 191 us  [the longest x8 135 us: lax.psum(lax.psum(shard_in, axis_name='dp'), 'expert')]
    psum x8, blocking collectives: 512 us -> 540 us  [one_tick(): logits = lax.psum(partial_logits, ('expert', 'dp'))]
where the time goes in v1:
time: 1210 us
  blocking collectives  1060 us (88%)
  matrix products  68.7 us (6%)
  waiting for transfers between devices  35.8 us (3%)
  local copies, waits for them, and re-layouts  20.9 us (2%)
  other arithmetic  16.5 us (1%)
    psum x8, blocking collectives, one_tick(): logits = lax.psum(partial_logits, ('expert', 'dp'))  540 us
    psum x8, blocking collectives, lax.psum(lax.psum(shard_in, axis_name='dp'), 'expert')  135 us
    all_to_all x8, blocking collectives, joined_work(): lax.all_to_all(expert_part.reshape(item_count, experts * lane_count, piec...  130 us
    all_to_all x8, blocking collectives, one_tick(): lax.all_to_all(spread.reshape(experts * lane_count, capacity, piece_width...  127 us
    psum x1, blocking collectives, per_device(): lax.psum((local_totals, local_counts), ('section', 'expert', 'dp'))  72.8 us
    psum x8, blocking collectives, lax.psum(shard_in, axis_name='dp')  56.3 us
    ppermute x8, waiting for transfers between devices, from_behind(): return lax.ppermute(value, axis, pairs)  35.8 us
    dot_general x8, matrix products, expert_rows(): jnp.dot(activated, down_matrix, preferred_element_type=jnp.float32)  35.4 us
  transfers between devices with their start and end apart: 8, of which 8 were waited for; matrix products, arithmetic and copies ran while one was open for 0% of the time, Pallas kernels for 0%

profile of v1, /device:TPU:1, one launch (start us, length us, event | category | flops | bytes accessed | tf_op | source)
XLA Modules:
  0.0 1207.1 jit_solution(6992363134999853861)
XLA Ops:
  2.3 1129.6 %while.17 = (s32[]{:T(128)}, bf16[256,128]{1,0:T(8,128)(2,1)S(1)}, s32[]{:T(128)}, s32[1,1,8,256,2]{3,4,2,1,0:T(2,128)}, f32[1,128]{1,0:T(1,128)}, /*index=5*/bf...) while((s32[]{:T(128)}, bf16[256,128]{1,0:T(8,128)(2,1)S(1)}, ...), condition=%wide.region_13.14_spmd.clone.clone, body=%wide.region_0.13_spmd.clone.clone.sunk | while | flops 947298944 | bytes 33645836 | solution.py:108
  12.5 18.9 %psum.68 = f32[256]{0:T(256)S(1)} all-reduce(f32[256]{0:T(256)S(1)} %psum.67), channel_id=1, replica_groups=mesh['section'=8,'expert'=8,'dp'=4] {'expert'}, use_global_device_ids=true, to_apply=%region_6.6 | all-reduce | flops 256 | bytes 2048 | tf_op jit(solution)/shard_map/while/body/eval_jaxpr/psum | solution.py:8
  32.3 68.4 %psum.69 = f32[256,8]{0,1:T(8,128)S(1)} all-reduce(f32[256,8]{0,1:T(8,128)S(1)} %fusion.93), channel_id=1, replica_groups=mesh['section'=8,'expert'=8,'dp'=4] {'expert','dp'}, use_global_device_ids=true, to_apply=%region_7.7 | all-reduce | flops 2048 | bytes 16384 | tf_op jit(solution)/shard_map/while/body/eval_jaxpr/psum | solution.py:70
  158.7 16.9 %psum.68 = f32[256]{0:T(256)S(1)} all-reduce(f32[256]{0:T(256)S(1)} %psum.67), channel_id=1, replica_groups=mesh['section'=8,'expert'=8,'dp'=4] {'expert'}, use_global_device_ids=true, to_apply=%region_6.6 | all-reduce | flops 256 | bytes 2048 | tf_op jit(solution)/shard_map/while/body/eval_jaxpr/psum | solution.py:8
  176.5 67.2 %psum.69 = f32[256,8]{0,1:T(8,128)S(1)} all-reduce(f32[256,8]{0,1:T(8,128)S(1)} %fusion.93), channel_id=1, replica_groups=mesh['section'=8,'expert'=8,'dp'=4] {'expert','dp'}, use_global_device_ids=true, to_apply=%region_7.7 | all-reduce | flops 2048 | bytes 16384 | tf_op jit(solution)/shard_map/while/body/eval_jaxpr/psum | solution.py:70
  268.3 16.2 %all_to_all.59 = bf16[72,32,128]{2,0,1:T(8,128)(2,1)S(1)} all-to-all(bf16[72,32,128]{2,0,1:T(8,128)(2,1)S(1)} %bitcast.119), channel_id=1, replica_groups=mesh['section'=8,'expert'=8,'dp'=4] {'expert','dp'}, dimensions={1} | all-to-all | bytes 1179648 | tf_op jit(solution)/shard_map/while/body/eval_jaxpr/all_to_all | solution.py:48
  299.1 16.5 %psum.68 = f32[256]{0:T(256)S(1)} all-reduce(f32[256]{0:T(256)S(1)} %psum.67), channel_id=1, replica_groups=mesh['section'=8,'expert'=8,'dp'=4] {'expert'}, use_global_device_ids=true, to_apply=%region_6.6 | all-reduce | flops 256 | bytes 2048 | tf_op jit(solution)/shard_map/while/body/eval_jaxpr/psum | solution.py:8
  316.6 67.4 %psum.69 = f32[256,8]{0,1:T(8,128)S(1)} all-reduce(f32[256,8]{0,1:T(8,128)S(1)} %fusion.93), channel_id=1, replica_groups=mesh['section'=8,'expert'=8,'dp'=4] {'expert','dp'}, use_global_device_ids=true, to_apply=%region_7.7 | all-reduce | flops 2048 | bytes 16384 | tf_op jit(solution)/shard_map/while/body/eval_jaxpr/psum | solution.py:70
  408.5 16.2 %all_to_all.59 = bf16[72,32,128]{2,0,1:T(8,128)(2,1)S(1)} all-to-all(bf16[72,32,128]{2,0,1:T(8,128)(2,1)S(1)} %bitcast.119), channel_id=1, replica_groups=mesh['section'=8,'expert'=8,'dp'=4] {'expert','dp'}, dimensions={1} | all-to-all | bytes 1179648 | tf_op jit(solution)/shard_map/while/body/eval_jaxpr/all_to_all | solution.py:48
  439.4 16.5 %psum.68 = f32[256]{0:T(256)S(1)} all-reduce(f32[256]{0:T(256)S(1)} %psum.67), channel_id=1, replica_groups=mesh['section'=8,'expert'=8,'dp'=4] {'expert'}, use_global_device_ids=true, to_apply=%region_6.6 | all-reduce | flops 256 | bytes 2048 | tf_op jit(solution)/shard_map/while/body/eval_jaxpr/psum | solution.py:8
  456.8 67.4 %psum.69 = f32[256,8]{0,1:T(8,128)S(1)} all-reduce(f32[256,8]{0,1:T(8,128)S(1)} %fusion.93), channel_id=1, replica_groups=mesh['section'=8,'expert'=8,'dp'=4] {'expert','dp'}, use_global_device_ids=true, to_apply=%region_7.7 | all-reduce | flops 2048 | bytes 16384 | tf_op jit(solution)/shard_map/while/body/eval_jaxpr/psum | solution.py:70
  548.8 16.2 %all_to_all.59 = bf16[72,32,128]{2,0,1:T(8,128)(2,1)S(1)} all-to-all(bf16[72,32,128]{2,0,1:T(8,128)(2,1)S(1)} %bitcast.119), channel_id=1, replica_groups=mesh['section'=8,'expert'=8,'dp'=4] {'expert','dp'}, dimensions={1} | all-to-all | bytes 1179648 | tf_op jit(solution)/shard_map/while/body/eval_jaxpr/all_to_all | solution.py:48
  579.6 16.5 %psum.68 = f32[256]{0:T(256)S(1)} all-reduce(f32[256]{0:T(256)S(1)} %psum.67), channel_id=1, replica_groups=mesh['section'=8,'expert'=8,'dp'=4] {'expert'}, use_global_device_ids=true, to_apply=%region_6.6 | all-reduce | flops 256 | bytes 2048 | tf_op jit(solution)/shard_map/while/body/eval_jaxpr/psum | solution.py:8
  597.1 67.4 %psum.69 = f32[256,8]{0,1:T(8,128)S(1)} all-reduce(f32[256,8]{0,1:T(8,128)S(1)} %fusion.93), channel_id=1, replica_groups=mesh['section'=8,'expert'=8,'dp'=4] {'expert','dp'}, use_global_device_ids=true, to_apply=%region_7.7 | all-reduce | flops 2048 | bytes 16384 | tf_op jit(solution)/shard_map/while/body/eval_jaxpr/psum | solution.py:70
  689.1 16.2 %all_to_all.59 = bf16[72,32,128]{2,0,1:T(8,128)(2,1)S(1)} all-to-all(bf16[72,32,128]{2,0,1:T(8,128)(2,1)S(1)} %bitcast.119), channel_id=1, replica_groups=mesh['section'=8,'expert'=8,'dp'=4] {'expert','dp'}, dimensions={1} | all-to-all | bytes 1179648 | tf_op jit(solution)/shard_map/while/body/eval_jaxpr/all_to_all | solution.py:48
  719.9 16.5 %psum.68 = f32[256]{0:T(256)S(1)} all-reduce(f32[256]{0:T(256)S(1)} %psum.67), channel_id=1, replica_groups=mesh['section'=8,'expert'=8,'dp'=4] {'expert'}, use_global_device_ids=true, to_apply=%region_6.6 | all-reduce | flops 256 | bytes 2048 | tf_op jit(solution)/shard_map/while/body/eval_jaxpr/psum | solution.py:8
  737.3 67.4 %psum.69 = f32[256,8]{0,1:T(8,128)S(1)} all-reduce(f32[256,8]{0,1:T(8,128)S(1)} %fusion.93), channel_id=1, replica_groups=mesh['section'=8,'expert'=8,'dp'=4] {'expert','dp'}, use_global_device_ids=true, to_apply=%region_7.7 | all-reduce | flops 2048 | bytes 16384 | tf_op jit(solution)/shard_map/while/body/eval_jaxpr/psum | solution.py:70
  829.3 16.2 %all_to_all.59 = bf16[72,32,128]{2,0,1:T(8,128)(2,1)S(1)} all-to-all(bf16[72,32,128]{2,0,1:T(8,128)(2,1)S(1)} %bitcast.119), channel_id=1, replica_groups=mesh['section'=8,'expert'=8,'dp'=4] {'expert','dp'}, dimensions={1} | all-to-all | bytes 1179648 | tf_op jit(solution)/shard_map/while/body/eval_jaxpr/all_to_all | solution.py:48
  860.2 16.5 %psum.68 = f32[256]{0:T(256)S(1)} all-reduce(f32[256]{0:T(256)S(1)} %psum.67), channel_id=1, replica_groups=mesh['section'=8,'expert'=8,'dp'=4] {'expert'}, use_global_device_ids=true, to_apply=%region_6.6 | all-reduce | flops 256 | bytes 2048 | tf_op jit(solution)/shard_map/while/body/eval_jaxpr/psum | solution.py:8
  877.6 67.4 %psum.69 = f32[256,8]{0,1:T(8,128)S(1)} all-reduce(f32[256,8]{0,1:T(8,128)S(1)} %fusion.93), channel_id=1, replica_groups=mesh['section'=8,'expert'=8,'dp'=4] {'expert','dp'}, use_global_device_ids=true, to_apply=%region_7.7 | all-reduce | flops 2048 | bytes 16384 | tf_op jit(solution)/shard_map/while/body/eval_jaxpr/psum | solution.py:70
  1000.4 16.5 %psum.68 = f32[256]{0:T(256)S(1)} all-reduce(f32[256]{0:T(256)S(1)} %psum.67), channel_id=1, replica_groups=mesh['section'=8,'expert'=8,'dp'=4] {'expert'}, use_global_device_ids=true, to_apply=%region_6.6 | all-reduce | flops 256 | bytes 2048 | tf_op jit(solution)/shard_map/while/body/eval_jaxpr/psum | solution.py:8
  1017.9 67.4 %psum.69 = f32[256,8]{0,1:T(8,128)S(1)} all-reduce(f32[256,8]{0,1:T(8,128)S(1)} %fusion.93), channel_id=1, replica_groups=mesh['section'=8,'expert'=8,'dp'=4] {'expert','dp'}, use_global_device_ids=true, to_apply=%region_7.7 | all-reduce | flops 2048 | bytes 16384 | tf_op jit(solution)/shard_map/while/body/eval_jaxpr/psum | solution.py:70
  1109.8 16.2 %all_to_all.59 = bf16[72,32,128]{2,0,1:T(8,128)(2,1)S(1)} all-to-all(bf16[72,32,128]{2,0,1:T(8,128)(2,1)S(1)} %bitcast.119), channel_id=1, replica_groups=mesh['section'=8,'expert'=8,'dp'=4] {'expert','dp'}, dimensions={1} | all-to-all | bytes 1179648 | tf_op jit(solution)/shard_map/while/body/eval_jaxpr/all_to_all | solution.py:48
  1132.1 72.8 %all-reduce = (f32[8]{0:T(128)S(1)}, f32[8]{0:T(128)S(1)}) all-reduce(f32[8]{0:T(128)S(1)} %broadcast_multiply_fusion.1, f32[8]{0:T(128)S(1)} %convolution_bitcast_fusion.1), channel_id=1, replica_groups=mesh['section'=8,'expert'=8,'dp'=4] {'section','expert','dp'}, use_global_device_ids=true, to_apply=%region_17.18 | all-reduce | flops 16 | bytes 128 | tf_op jit(solution)/shard_map/psum | solution.py:117
  (305 shorter events, 360.1 us)
Async XLA Ops:
  2.3 1129.6 %copy-start.1 = (bf16[1,256,128]{2,1,0:T(8,128)(2,1)S(1)}, bf16[1,256,128]{2,1,0:T(8,128)(2,1)}, u32[]{:S(2)}) copy-start(bf16[1,256,128]{2,1,0:T(8,128)(2,1)} %param.12) | copy-start | bytes 196612
  2.3 1129.7 %copy-start.3 = (s32[1,256]{1,0:T(1,128)S(1)}, s32[1,256]{1,0:T(1,128)}, u32[]{:S(2)}) copy-start(s32[1,256]{1,0:T(1,128)} %param.13) | copy-start | bytes 3076
  102.5 17.4 %copy-start = (bf16[4096,384]{1,0:T(8,128)(2,1)S(1)}, bf16[4096,384]{1,0:T(8,128)(2,1)}, u32[]{:S(2)}) copy-start(bf16[4096,384]{1,0:T(8,128)(2,1)} %get-tuple-element.482) | copy-start | bytes 9437188 | tf_op jit(solution)/shard_map/while
  142.9 7.3 collective-permute-start
  245.5 17.4 %copy-start = (bf16[4096,384]{1,0:T(8,128)(2,1)S(1)}, bf16[4096,384]{1,0:T(8,128)(2,1)}, u32[]{:S(2)}) copy-start(bf16[4096,384]{1,0:T(8,128)(2,1)} %get-tuple-element.482) | copy-start | bytes 9437188 | tf_op jit(solution)/shard_map/while
  285.9 4.4 collective-permute-start
  385.8 17.4 %copy-start = (bf16[4096,384]{1,0:T(8,128)(2,1)S(1)}, bf16[4096,384]{1,0:T(8,128)(2,1)}, u32[]{:S(2)}) copy-start(bf16[4096,384]{1,0:T(8,128)(2,1)} %get-tuple-element.482) | copy-start | bytes 9437188 | tf_op jit(solution)/shard_map/while
  426.1 4.4 collective-permute-start
  526.0 17.4 %copy-start = (bf16[4096,384]{1,0:T(8,128)(2,1)S(1)}, bf16[4096,384]{1,0:T(8,128)(2,1)}, u32[]{:S(2)}) copy-start(bf16[4096,384]{1,0:T(8,128)(2,1)} %get-tuple-element.482) | copy-start | bytes 9437188 | tf_op jit(solution)/shard_map/while
  566.4 4.4 collective-permute-start
  666.3 17.4 %copy-start = (bf16[4096,384]{1,0:T(8,128)(2,1)S(1)}, bf16[4096,384]{1,0:T(8,128)(2,1)}, u32[]{:S(2)}) copy-start(bf16[4096,384]{1,0:T(8,128)(2,1)} %get-tuple-element.482) | copy-start | bytes 9437188 | tf_op jit(solution)/shard_map/while
  706.7 4.4 collective-permute-start
  806.6 17.4 %copy-start = (bf16[4096,384]{1,0:T(8,128)(2,1)S(1)}, bf16[4096,384]{1,0:T(8,128)(2,1)}, u32[]{:S(2)}) copy-start(bf16[4096,384]{1,0:T(8,128)(2,1)} %get-tuple-element.482) | copy-start | bytes 9437188 | tf_op jit(solution)/shard_map/while
  846.9 4.4 collective-permute-start
  946.8 17.4 %copy-start = (bf16[4096,384]{1,0:T(8,128)(2,1)S(1)}, bf16[4096,384]{1,0:T(8,128)(2,1)}, u32[]{:S(2)}) copy-start(bf16[4096,384]{1,0:T(8,128)(2,1)} %get-tuple-element.482) | copy-start | bytes 9437188 | tf_op jit(solution)/shard_map/while
  987.2 4.4 collective-permute-start
  1087.1 17.4 %copy-start = (bf16[4096,384]{1,0:T(8,128)(2,1)S(1)}, bf16[4096,384]{1,0:T(8,128)(2,1)}, u32[]{:S(2)}) copy-start(bf16[4096,384]{1,0:T(8,128)(2,1)} %get-tuple-element.482) | copy-start | bytes 9437188 | tf_op jit(solution)/shard_map/while
  1127.4 4.4 collective-permute-start
  1205.5 1.5 copy-start.2
